TPU v7x, 32 devices: a whole 2x2x4 slice. The times are simulated.
32 devices in a mesh: mom: 4 (over z), en: 2 (over y), atom: 4 (over x, core).
Axes of the slice: x: 2, y: 2, z: 4, core: 2. Of those that a mesh axis runs over, the one named last changes fastest.
Arguments:
- green_blocks: bfloat16 [16, 12, 16, 2, 128, 128], P('mom', 'en', 'atom'), may hold values from -6 to 6
- coupling: bfloat16 [4, 16, 4, 128, 128], P(None, 'atom'), may hold values from -0.25 to 0.25
- neighbours: int32 [16, 4], P('atom'), may hold values from 0 to 15, as said below
- momentum_shift: int32 [4], replicated, may hold values from -2 to 2, as said below
- energy_offset: int32 [4], replicated, may hold values from 1 to 2, as said below
- phonon_weight: float32 [4], replicated, may hold values from 0.3 to 1.5
Outputs:
- self_energy: float32 [16, 12, 16, 2, 128, 128], P('mom', 'en', 'atom')
Inputs may be any that keep to these rules, and one draw needn't show every extreme that they name: `neighbours`: cluster a is bonded to (a + 2) mod 16 and (a - 2) mod 16; each other bond is to (a + d) mod 16 with d between -2 and 2. `momentum_shift`: the transfers 2 and -2 both occur. `energy_offset`: the offsets 1 and 2 both occur.
All inputs are finite; a program needn't handle non-finite values.
Results may differ from a plain program's by a relative error of at most 0.0029.
Values may be sent and summed in bfloat16 or wider, within the bound.
A program may use at most 192 MiB of HBM per device.

v0:
```python
import jax
import jax.numpy as jnp
from jax import lax
from jax.sharding import PartitionSpec as P

REACH = 2
OFFMAX = 2


def with_halo(cells, sides, width):
    for axis, dim in sides:
        count = lax.axis_size(axis)
        head = lax.slice_in_dim(cells, 0, width, axis=dim)
        tail = lax.slice_in_dim(cells, cells.shape[dim] - width, cells.shape[dim], axis=dim)
        cells = jnp.concatenate(
            [
                lax.ppermute(tail, axis, [(i, (i + 1) % count) for i in range(count)]),
                cells,
                lax.ppermute(head, axis, [((i + 1) % count, i) for i in range(count)]),
            ],
            axis=dim,
        )
    return cells


def from_behind(value, axis, steps):
    count = lax.axis_size(axis)
    leading, last = (max(0, -steps), min(count, count - steps))
    return lax.ppermute(value, axis, [(source, source + steps) for source in range(leading, last)])


def extend_blocks(green_blocks):
    return with_halo(green_blocks, (("mom", 0), ("atom", 2)), REACH)


def send_upward(upper_terms):
    return from_behind(upper_terms, "en", 1)


def block_terms(extended, coupling, mom_rows, cluster_rows, first_energy, energy_span):
    window = lax.slice_in_dim(extended, first_energy, first_energy + energy_span, axis=1)

    def one_momentum(moment_index):
        chosen = jnp.take(window, mom_rows[moment_index], axis=0)
        picked = jnp.take(chosen, cluster_rows, axis=2)
        left_products = jnp.einsum(
            "tajxy,teajryz->teajrxz", coupling, picked, preferred_element_type=jnp.float32
        ).astype(jnp.bfloat16)
        return jnp.einsum(
            "teajrxz,tajwz->earxw", left_products, coupling, preferred_element_type=jnp.float32
        )

    return lax.map(one_momentum, jnp.arange(mom_rows.shape[0], dtype=jnp.int32))


def per_device(green_blocks, coupling, neighbours, momentum_shift, energy_offset, phonon_weight):
    mom_local = green_blocks.shape[0]
    energy_local = green_blocks.shape[1]
    cluster_local = green_blocks.shape[2]
    all_clusters = cluster_local * lax.axis_size("atom")
    extended = extend_blocks(green_blocks)
    mom_rows = jnp.arange(mom_local, dtype=jnp.int32)[:, None] + REACH - momentum_shift[None, :]
    global_rows = lax.axis_index("atom") * cluster_local + jnp.arange(
        cluster_local, dtype=jnp.int32
    )
    distance = (neighbours - global_rows[:, None] + REACH) % all_clusters - REACH
    cluster_rows = jnp.arange(cluster_local, dtype=jnp.int32)[:, None] + REACH + distance
    upper_terms = block_terms(
        extended, coupling, mom_rows, cluster_rows, energy_local - OFFMAX, OFFMAX
    )
    lower = send_upward(upper_terms)
    rest_terms = block_terms(extended, coupling, mom_rows, cluster_rows, 0, energy_local - OFFMAX)
    scattering_terms = jnp.concatenate([rest_terms, upper_terms], axis=1)
    joined = jnp.concatenate([lower, scattering_terms], axis=1)
    source_index = jnp.arange(energy_local + OFFMAX, dtype=jnp.int32)[None, None, :]
    target_index = jnp.arange(energy_local, dtype=jnp.int32)[None, :, None]
    matches = source_index == target_index + OFFMAX - energy_offset[:, None, None]
    spread = jnp.sum(phonon_weight[:, None, None] * matches.astype(jnp.float32), axis=0)
    return jnp.einsum("es,ksarxw->kearxw", spread, joined, precision=lax.Precision.HIGHEST)


def solution(mesh):
    return jax.shard_map(
        per_device,
        mesh=mesh,
        in_specs=(
            P("mom", "en", "atom", None, None, None),
            P(None, "atom", None, None, None),
            P("atom", None),
            P(),
            P(),
            P(),
        ),
        out_specs=P("mom", "en", "atom", None, None, None),
        check_vma=False,
    )
```

profile of v0, /device:TPU:0, one launch (start us, length us, event | category | flops | bytes accessed | tf_op | source)
XLA Modules:
  0.0 718.7 jit_solution(8134069025559666933)
XLA Ops:
  0.0 6.7 fusion.56
  11.7 69.0 %collective-permute-done = bf16[2,6,4,2,128,128]{5,4,3,2,1,0:T(8,128)(2,1)S(1)} collective-permute-done((bf16[2,6,4,2,128,128]{5,4,3,2,1,0:T(8,128)(2,1)S(1)}, bf16[2,6,4,2,128,128]{5,4,3,2,1,0:T(8,128)(2,1)S(1)}, u32[]{:S(2)}, u32[]{:S(2)}) %collective-permute-start) | collective-permute-done | bytes 3145760 | tf_op jit(solution)/shard_map/ppermute | solution.py:17
  82.7 64.3 %collective-permute-done.1 = bf16[2,6,4,2,128,128]{5,4,3,2,1,0:T(8,128)(2,1)} collective-permute-done((bf16[2,6,4,2,128,128]{5,4,3,2,1,0:T(8,128)(2,1)}, bf16[2,6,4,2,128,128]{5,4,3,2,1,0:T(8,128)(2,1)}, u32[]{:S(2)}, u32[]{:S(2)}) %collective-permute-start.1) | collective-permute-done | bytes 3145760 | tf_op jit(solution)/shard_map/ppermute | solution.py:19
  149.6 5.7 fusion.55
  161.4 133.8 %collective-permute-done.3 = bf16[8,6,2,2,128,128]{5,4,3,2,1,0:T(8,128)(2,1)} collective-permute-done((bf16[8,6,2,2,128,128]{5,4,3,2,1,0:T(8,128)(2,1)}, bf16[8,6,2,2,128,128]{5,4,3,2,1,0:T(8,128)(2,1)}, u32[]{:S(2)}, u32[]{:S(2)}) %collective-permute-start.3) | collective-permute-done | bytes 6291488 | tf_op jit(solution)/shard_map/ppermute | solution.py:19
  296.5 7.1 pad_maximum_fusion.2
  303.6 126.0 %while.22 = (s32[]{:T(128)}, f32[4,2,4,2,128,128]{5,1,4,3,2,0:T(2,128)}, s32[4,4]{1,0:T(4,128)S(1)}, s32[4]{0:T(128)S(1)}, s32[4,4]{1,0:T(4,128)S(1)}, /*index=5...) while((s32[]{:T(128)}, ...), condition=%wide.region_1.2_spmd, body=%wide.region_0.1_spmd.sunk | while | flops 2157971712 | bytes 47194844 | solution.py:53
  305.9 6.4 gather_fusion
  312.3 4.6 broadcast_select_fusion.4
  317.0 6.9 gather_fusion.1
  323.9 9.3 %fusion.73 = f32[1,2,4,2,128,128]{5,4,3,1,2,0:T(8,128)S(1)} fusion(bf16[4,4,4,128,128]{4,3,0,2,1:T(8,128)(2,1)} %get-tuple-element.324, bf16[4,4,4,2,2,128,128]{6,5,4,3,2,1,0:T(8,128)(2,1)} %bitcast.131, pred[4,4]{1,0:T(4,128)(4,1)S(1)} %compare_and_fusion.9), kind=kOutput, calls=%fused_computation.13.clone.1 | convolution fusion | flops 2155872256 | bytes 11534352 | tf_op jit(solution)/shard_map/while/body/eval_jaxpr/teajrxz,tajwz->earxw/dot_general | solution.py:49
  337.4 6.4 gather_fusion
  343.8 4.6 broadcast_select_fusion.4
  348.5 6.9 gather_fusion.1
  355.4 9.3 %fusion.73 = f32[1,2,4,2,128,128]{5,4,3,1,2,0:T(8,128)S(1)} fusion(bf16[4,4,4,128,128]{4,3,0,2,1:T(8,128)(2,1)} %get-tuple-element.324, bf16[4,4,4,2,2,128,128]{6,5,4,3,2,1,0:T(8,128)(2,1)} %bitcast.131, pred[4,4]{1,0:T(4,128)(4,1)S(1)} %compare_and_fusion.9), kind=kOutput, calls=%fused_computation.13.clone.1 | convolution fusion | flops 2155872256 | bytes 11534352 | tf_op jit(solution)/shard_map/while/body/eval_jaxpr/teajrxz,tajwz->earxw/dot_general | solution.py:49
  368.9 6.4 gather_fusion
  375.3 4.6 broadcast_select_fusion.4
  380.0 6.9 gather_fusion.1
  386.9 9.3 %fusion.73 = f32[1,2,4,2,128,128]{5,4,3,1,2,0:T(8,128)S(1)} fusion(bf16[4,4,4,128,128]{4,3,0,2,1:T(8,128)(2,1)} %get-tuple-element.324, bf16[4,4,4,2,2,128,128]{6,5,4,3,2,1,0:T(8,128)(2,1)} %bitcast.131, pred[4,4]{1,0:T(4,128)(4,1)S(1)} %compare_and_fusion.9), kind=kOutput, calls=%fused_computation.13.clone.1 | convolution fusion | flops 2155872256 | bytes 11534352 | tf_op jit(solution)/shard_map/while/body/eval_jaxpr/teajrxz,tajwz->earxw/dot_general | solution.py:49
  400.3 6.4 gather_fusion
  406.8 4.6 broadcast_select_fusion.4
  411.5 6.9 gather_fusion.1
  418.4 9.3 %fusion.73 = f32[1,2,4,2,128,128]{5,4,3,1,2,0:T(8,128)S(1)} fusion(bf16[4,4,4,128,128]{4,3,0,2,1:T(8,128)(2,1)} %get-tuple-element.324, bf16[4,4,4,2,2,128,128]{6,5,4,3,2,1,0:T(8,128)(2,1)} %bitcast.131, pred[4,4]{1,0:T(4,128)(4,1)S(1)} %compare_and_fusion.9), kind=kOutput, calls=%fused_computation.13.clone.1 | convolution fusion | flops 2155872256 | bytes 11534352 | tf_op jit(solution)/shard_map/while/body/eval_jaxpr/teajrxz,tajwz->earxw/dot_general | solution.py:49
  429.6 5.4 collective-permute-start.4
  434.9 13.8 %pad_maximum_fusion = bf16[8,4,8,2,128,128]{5,4,3,2,1,0:T(8,128)(2,1)} fusion(bf16[8,6,2,2,128,128]{5,4,3,2,1,0:T(8,128)(2,1)} %collective-permute-done.3, bf16[8,6,4,2,128,128]{5,4,3,2,1,0:T(8,128)(2,1)} %copy-done, bf16[8,6,2,2,128,128]{5,4,3,2,1,0:T(8,128)(2,1)} %collective-permute-done.2), kind=kLoop, calls=%fused_computation.43 | loop fusion | flops 16777216 | bytes 41943040 | tf_op jit(solution)/shard_map/concatenate | solution.py:15
  448.7 231.4 %while.24 = (s32[]{:T(128)}, f32[4,4,4,2,128,128]{5,1,4,3,2,0:T(4,128)}, s32[4,4]{1,0:T(4,128)S(1)}, s32[4]{0:T(128)S(1)}, s32[4,4]{1,0:T(4,128)S(1)}, /*index=5...) while((s32[]{:T(128)}, ...), condition=%wide.region_3.4_spmd, body=%wide.region_2.3_spmd.sunk | while | flops 4315939840 | bytes 79697232 | solution.py:53
  451.3 17.9 %while.25 = (s32[]{:T(128)}, bf16[8,4,8,2,128,128]{5,4,3,2,1,0:T(8,128)(2,1)}, s32[4,1]{0,1:T(1,128)S(1)}, bf16[4,4,8,2,128,128]{5,4,3,2,1,0:T(8,128)(2,1)}, s32[]{:T(128)}) while((s32[]{:T(128)}, bf16[8,4,8,2,128,128]{5,4,3,2,1,0:T(8,128)(2,1)}, s32[4,1]{0,1:T(1,128)S(1)}, bf16[4,4,8,2,128,128]{5,4,3,2,1,0:T(8,128)(2,1)}, s32[]{:T(128)}) %tuple.54), condition=%wide.while_cond, body=%wide.while_body.sunk | while | flops 2 | bytes 4194901 | solution.py:44
  451.9 3.8 dynamic-slice_dynamic-update-slice_fusion.2
  456.4 3.8 dynamic-slice_dynamic-update-slice_fusion.2
  460.9 3.8 dynamic-slice_dynamic-update-slice_fusion.2
  469.2 7.6 %broadcast_select_fusion.5 = bf16[4,4,8,2,128,128]{5,4,3,2,1,0:T(8,128)(2,1)} fusion(bf16[4,4,8,2,128,128]{5,4,3,2,1,0:T(8,128)(2,1)} %get-tuple-element.277, pred[4]{0:T(512)(128)(4,1)S(1)} %compare_and_fusion.10), kind=kLoop, calls=%fused_computation.31.clone.1 | loop fusion | flops 4194304 | bytes 16777220 | tf_op jit(solution)/shard_map/while/body/eval_jaxpr/jit(_take)/select_n | solution.py:44
  476.9 10.6 %gather_fusion.2 = bf16[16,4,4,2,128,128]{5,4,3,2,1,0:T(8,128)(2,1)} fusion(bf16[4,4,8,2,128,128]{5,4,3,2,1,0:T(8,128)(2,1)} %broadcast_select_fusion.5, s32[1024]{0:T(1024)S(1)} %pad_clamp_fusion.8), kind=kCustom, calls=%fused_computation.2.clone.1 | custom fusion | bytes 33554496 | tf_op jit(solution)/shard_map/while/body/eval_jaxpr/jit(_take)/gather | solution.py:45
  487.6 16.2 %fusion.78 = f32[1,4,4,2,128,128]{5,4,3,1,2,0:T(8,128)S(1)} fusion(bf16[4,4,4,128,128]{4,3,0,2,1:T(8,128)(2,1)} %get-tuple-element.356, bf16[4,4,4,4,2,128,128]{6,5,4,3,2,1,0:T(8,128)(2,1)} %bitcast.130, pred[4,4]{1,0:T(4,128)(4,1)S(1)} %compare_and_fusion.11), kind=kOutput, calls=%fused_computation.34.clone.1 | convolution fusion | flops 4311744512 | bytes 20971536 | tf_op jit(solution)/shard_map/while/body/eval_jaxpr/teajrxz,tajwz->earxw/dot_general | solution.py:49
  509.1 17.9 %while.25 = (s32[]{:T(128)}, bf16[8,4,8,2,128,128]{5,4,3,2,1,0:T(8,128)(2,1)}, s32[4,1]{0,1:T(1,128)S(1)}, bf16[4,4,8,2,128,128]{5,4,3,2,1,0:T(8,128)(2,1)}, s32[]{:T(128)}) while((s32[]{:T(128)}, bf16[8,4,8,2,128,128]{5,4,3,2,1,0:T(8,128)(2,1)}, s32[4,1]{0,1:T(1,128)S(1)}, bf16[4,4,8,2,128,128]{5,4,3,2,1,0:T(8,128)(2,1)}, s32[]{:T(128)}) %tuple.54), condition=%wide.while_cond, body=%wide.while_body.sunk | while | flops 2 | bytes 4194901 | solution.py:44
  527.0 7.6 %broadcast_select_fusion.5 = bf16[4,4,8,2,128,128]{5,4,3,2,1,0:T(8,128)(2,1)} fusion(bf16[4,4,8,2,128,128]{5,4,3,2,1,0:T(8,128)(2,1)} %get-tuple-element.277, pred[4]{0:T(512)(128)(4,1)S(1)} %compare_and_fusion.10), kind=kLoop, calls=%fused_computation.31.clone.1 | loop fusion | flops 4194304 | bytes 16777220 | tf_op jit(solution)/shard_map/while/body/eval_jaxpr/jit(_take)/select_n | solution.py:44
  534.8 10.6 %gather_fusion.2 = bf16[16,4,4,2,128,128]{5,4,3,2,1,0:T(8,128)(2,1)} fusion(bf16[4,4,8,2,128,128]{5,4,3,2,1,0:T(8,128)(2,1)} %broadcast_select_fusion.5, s32[1024]{0:T(1024)S(1)} %pad_clamp_fusion.8), kind=kCustom, calls=%fused_computation.2.clone.1 | custom fusion | bytes 33554496 | tf_op jit(solution)/shard_map/while/body/eval_jaxpr/jit(_take)/gather | solution.py:45
  545.4 16.2 %fusion.78 = f32[1,4,4,2,128,128]{5,4,3,1,2,0:T(8,128)S(1)} fusion(bf16[4,4,4,128,128]{4,3,0,2,1:T(8,128)(2,1)} %get-tuple-element.356, bf16[4,4,4,4,2,128,128]{6,5,4,3,2,1,0:T(8,128)(2,1)} %bitcast.130, pred[4,4]{1,0:T(4,128)(4,1)S(1)} %compare_and_fusion.11), kind=kOutput, calls=%fused_computation.34.clone.1 | convolution fusion | flops 4311744512 | bytes 20971536 | tf_op jit(solution)/shard_map/while/body/eval_jaxpr/teajrxz,tajwz->earxw/dot_general | solution.py:49
  567.0 17.9 %while.25 = (s32[]{:T(128)}, bf16[8,4,8,2,128,128]{5,4,3,2,1,0:T(8,128)(2,1)}, s32[4,1]{0,1:T(1,128)S(1)}, bf16[4,4,8,2,128,128]{5,4,3,2,1,0:T(8,128)(2,1)}, s32[]{:T(128)}) while((s32[]{:T(128)}, bf16[8,4,8,2,128,128]{5,4,3,2,1,0:T(8,128)(2,1)}, s32[4,1]{0,1:T(1,128)S(1)}, bf16[4,4,8,2,128,128]{5,4,3,2,1,0:T(8,128)(2,1)}, s32[]{:T(128)}) %tuple.54), condition=%wide.while_cond, body=%wide.while_body.sunk | while | flops 2 | bytes 4194901 | solution.py:44
  584.9 7.6 %broadcast_select_fusion.5 = bf16[4,4,8,2,128,128]{5,4,3,2,1,0:T(8,128)(2,1)} fusion(bf16[4,4,8,2,128,128]{5,4,3,2,1,0:T(8,128)(2,1)} %get-tuple-element.277, pred[4]{0:T(512)(128)(4,1)S(1)} %compare_and_fusion.10), kind=kLoop, calls=%fused_computation.31.clone.1 | loop fusion | flops 4194304 | bytes 16777220 | tf_op jit(solution)/shard_map/while/body/eval_jaxpr/jit(_take)/select_n | solution.py:44
  592.7 10.6 %gather_fusion.2 = bf16[16,4,4,2,128,128]{5,4,3,2,1,0:T(8,128)(2,1)} fusion(bf16[4,4,8,2,128,128]{5,4,3,2,1,0:T(8,128)(2,1)} %broadcast_select_fusion.5, s32[1024]{0:T(1024)S(1)} %pad_clamp_fusion.8), kind=kCustom, calls=%fused_computation.2.clone.1 | custom fusion | bytes 33554496 | tf_op jit(solution)/shard_map/while/body/eval_jaxpr/jit(_take)/gather | solution.py:45
  603.3 16.2 %fusion.78 = f32[1,4,4,2,128,128]{5,4,3,1,2,0:T(8,128)S(1)} fusion(bf16[4,4,4,128,128]{4,3,0,2,1:T(8,128)(2,1)} %get-tuple-element.356, bf16[4,4,4,4,2,128,128]{6,5,4,3,2,1,0:T(8,128)(2,1)} %bitcast.130, pred[4,4]{1,0:T(4,128)(4,1)S(1)} %compare_and_fusion.11), kind=kOutput, calls=%fused_computation.34.clone.1 | convolution fusion | flops 4311744512 | bytes 20971536 | tf_op jit(solution)/shard_map/while/body/eval_jaxpr/teajrxz,tajwz->earxw/dot_general | solution.py:49
  624.8 17.9 %while.25 = (s32[]{:T(128)}, bf16[8,4,8,2,128,128]{5,4,3,2,1,0:T(8,128)(2,1)}, s32[4,1]{0,1:T(1,128)S(1)}, bf16[4,4,8,2,128,128]{5,4,3,2,1,0:T(8,128)(2,1)}, s32[]{:T(128)}) while((s32[]{:T(128)}, bf16[8,4,8,2,128,128]{5,4,3,2,1,0:T(8,128)(2,1)}, s32[4,1]{0,1:T(1,128)S(1)}, bf16[4,4,8,2,128,128]{5,4,3,2,1,0:T(8,128)(2,1)}, s32[]{:T(128)}) %tuple.54), condition=%wide.while_cond, body=%wide.while_body.sunk | while | flops 2 | bytes 4194901 | solution.py:44
  629.9 3.8 dynamic-slice_dynamic-update-slice_fusion.2
  642.7 7.6 %broadcast_select_fusion.5 = bf16[4,4,8,2,128,128]{5,4,3,2,1,0:T(8,128)(2,1)} fusion(bf16[4,4,8,2,128,128]{5,4,3,2,1,0:T(8,128)(2,1)} %get-tuple-element.277, pred[4]{0:T(512)(128)(4,1)S(1)} %compare_and_fusion.10), kind=kLoop, calls=%fused_computation.31.clone.1 | loop fusion | flops 4194304 | bytes 16777220 | tf_op jit(solution)/shard_map/while/body/eval_jaxpr/jit(_take)/select_n | solution.py:44
  650.5 10.6 %gather_fusion.2 = bf16[16,4,4,2,128,128]{5,4,3,2,1,0:T(8,128)(2,1)} fusion(bf16[4,4,8,2,128,128]{5,4,3,2,1,0:T(8,128)(2,1)} %broadcast_select_fusion.5, s32[1024]{0:T(1024)S(1)} %pad_clamp_fusion.8), kind=kCustom, calls=%fused_computation.2.clone.1 | custom fusion | bytes 33554496 | tf_op jit(solution)/shard_map/while/body/eval_jaxpr/jit(_take)/gather | solution.py:45
  661.1 16.2 %fusion.78 = f32[1,4,4,2,128,128]{5,4,3,1,2,0:T(8,128)S(1)} fusion(bf16[4,4,4,128,128]{4,3,0,2,1:T(8,128)(2,1)} %get-tuple-element.356, bf16[4,4,4,4,2,128,128]{6,5,4,3,2,1,0:T(8,128)(2,1)} %bitcast.130, pred[4,4]{1,0:T(4,128)(4,1)S(1)} %compare_and_fusion.11), kind=kOutput, calls=%fused_computation.34.clone.1 | convolution fusion | flops 4311744512 | bytes 20971536 | tf_op jit(solution)/shard_map/while/body/eval_jaxpr/teajrxz,tajwz->earxw/dot_general | solution.py:49
  680.1 25.8 %fusion.47 = f32[4,6,4,2,128,128]{5,1,4,3,2,0:T(8,128)} fusion(f32[4,2,4,2,128,128]{5,1,4,3,2,0:T(2,128)} %get-tuple-element.79, f32[4,4,4,2,128,128]{5,1,4,3,2,0:T(4,128)} %get-tuple-element.80, f32[4,2,4,2,128,128]{5,1,4,3,2,0:T(2,128)} %collective-permute-done.4, f32[6,8]{1,0:T(8,128)S(1)} %copy-done.3), kind=kOutput, calls=%fused_computation.51 | convolution fusion | flops 310378496 | bytes 29360320 | tf_op jit(solution)/shard_map/es,ksarxw->kearxw/dot_general | solution.py:79
  705.9 12.8 %copy.18 = f32[4,6,4,2,128,128]{5,4,3,2,1,0:T(8,128)} copy(f32[4,6,4,2,128,128]{5,1,4,3,2,0:T(8,128)} %fusion.47) | data formatting | bytes 25165824 | tf_op jit(solution)/shard_map/es,ksarxw->kearxw/transpose | solution.py:79
  (135 shorter events, 97.1 us)
Async XLA Ops:
  0.0 81.0 %copy-start.1 = (bf16[4,6,4,2,128,128]{5,4,3,2,1,0:T(8,128)(2,1)S(1)}, bf16[4,6,4,2,128,128]{5,4,3,2,1,0:T(8,128)(2,1)}, u32[]{:S(2)}) copy-start(bf16[4,6,4,2,128,128]{5,4,3,2,1,0:T(8,128)(2,1)} %param.10) | copy-start | bytes 18874372
  6.7 74.1 %collective-permute-start = (bf16[2,6,4,2,128,128]{5,4,3,2,1,0:T(8,128)(2,1)S(1)}, bf16[2,6,4,2,128,128]{5,4,3,2,1,0:T(8,128)(2,1)S(1)}, u32[]{:S(2)}, u32[]{:S(2)}) collective-permute-start(bf16[2,6,4,2,128,128]{5,4,3,2,1,0:T(8,128)(2,1)S(1)} %get-tuple-element.156), channel_id=1, source_target_pairs={{0,8},{8,16},{16,24},{24,0},{1,9},{9,17},{17,25},{25,1},{2,10},{10... | collective-permute-start | bytes 9437192 | tf_op jit(solution)/shard_map/ppermute | solution.py:17
  9.7 137.3 %collective-permute-start.1 = (bf16[2,6,4,2,128,128]{5,4,3,2,1,0:T(8,128)(2,1)}, bf16[2,6,4,2,128,128]{5,4,3,2,1,0:T(8,128)(2,1)}, u32[]{:S(2)}, u32[]{:S(2)}) collective-permute-start(bf16[2,6,4,2,128,128]{5,4,3,2,1,0:T(8,128)(2,1)} %get-tuple-element.155), channel_id=1, source_target_pairs={{8,0},{16,8},{24,16},{0,24},{9,1},{17,9},{25,17},{1,25},{10,2},{18... | collective-permute-start | bytes 9437192 | tf_op jit(solution)/shard_map/ppermute | solution.py:19
  149.5 8.8 %copy-start = (bf16[8,6,4,2,128,128]{5,4,3,2,1,0:T(8,128)(2,1)}, bf16[8,6,4,2,128,128]{5,4,3,2,1,0:T(8,128)(2,1)S(1)}, u32[]{:S(2)}) copy-start(bf16[8,6,4,2,128,128]{5,4,3,2,1,0:T(8,128)(2,1)S(1)} %constant_dynamic-update-slice_fusion) | copy-start | bytes 37748740
  149.5 9.5 %copy-start.2 = (bf16[4,4,4,128,128]{4,3,2,1,0:T(8,128)(2,1)S(1)}, bf16[4,4,4,128,128]{4,3,2,1,0:T(8,128)(2,1)}, u32[]{:S(2)}) copy-start(bf16[4,4,4,128,128]{4,3,2,1,0:T(8,128)(2,1)} %param.11) | copy-start | bytes 6291460
  149.5 11.0 %copy-start.5 = (s32[4]{0:T(128)S(1)}, s32[4]{0:T(128)}, u32[]{:S(2)}) copy-start(s32[4]{0:T(128)} %param.14) | copy-start | bytes 52
  149.5 11.1 %copy-start.6 = (f32[4]{0:T(128)S(1)}, f32[4]{0:T(128)}, u32[]{:S(2)}) copy-start(f32[4]{0:T(128)} %param.15) | copy-start | bytes 52
  149.6 11.7 %copy-start.4 = (s32[4,4]{1,0:T(4,128)S(1)}, s32[4,4]{1,0:T(4,128)}, u32[]{:S(2)}) copy-start(s32[4,4]{1,0:T(4,128)} %param.12) | copy-start | bytes 196
  149.6 11.7 %copy-start.7 = (s32[4]{0:T(128)S(1)}, s32[4]{0:T(128)}, u32[]{:S(2)}) copy-start(s32[4]{0:T(128)} %param.13) | copy-start | bytes 52
  158.3 136.8 %collective-permute-start.3 = (bf16[8,6,2,2,128,128]{5,4,3,2,1,0:T(8,128)(2,1)}, bf16[8,6,2,2,128,128]{5,4,3,2,1,0:T(8,128)(2,1)}, u32[]{:S(2)}, u32[]{:S(2)}) collective-permute-start(bf16[8,6,2,2,128,128]{5,4,3,2,1,0:T(8,128)(2,1)} %get-tuple-element.154), channel_id=1, source_target_pairs={{1,0},{2,1},{3,2},{0,3},{5,4},{6,5},{7,6},{4,7},{9,8},{10,9},{11,1... | collective-permute-start | bytes 18874376 | tf_op jit(solution)/shard_map/ppermute | solution.py:19
  159.1 137.4 %collective-permute-start.2 = (bf16[8,6,2,2,128,128]{5,4,3,2,1,0:T(8,128)(2,1)}, bf16[8,6,2,2,128,128]{5,4,3,2,1,0:T(8,128)(2,1)}, u32[]{:S(2)}, u32[]{:S(2)}) collective-permute-start(bf16[8,6,2,2,128,128]{5,4,3,2,1,0:T(8,128)(2,1)} %get-tuple-element.153), channel_id=1, source_target_pairs={{0,1},{1,2},{2,3},{3,0},{4,5},{5,6},{6,7},{7,4},{8,9},{9,10},{10,1... | collective-permute-start | bytes 18874376 | tf_op jit(solution)/shard_map/ppermute | solution.py:17
  429.6 250.5 %collective-permute-start.4 = (f32[4,2,4,2,128,128]{5,1,4,3,2,0:T(2,128)}, f32[4,2,4,2,128,128]{5,1,4,3,2,0:T(2,128)}, u32[]{:S(2)}, u32[]{:S(2)}) collective-permute-start(f32[4,2,4,2,128,128]{5,1,4,3,2,0:T(2,128)} %get-tuple-element.79), channel_id=1, source_target_pairs={{0,4},{1,5},{2,6},{3,7},{8,12},{9,13},{10,14},{11,15},{16,20},{17,... | collective-permute-start | bytes 12582920 | tf_op jit(solution)/shard_map/ppermute | solution.py:29
  448.7 231.4 %copy-start.3 = (f32[6,8]{1,0:T(8,128)S(1)}, f32[6,8]{1,0:T(8,128)}, u32[]{:S(2)}) copy-start(f32[6,8]{1,0:T(8,128)} %select_reduce_fusion) | copy-start | bytes 580
where the time goes:
time: 721 us; the launch traced here: 719 us
  waiting for transfers between devices  268 us (37%)
  local copies, waits for them, and re-layouts  225 us (31%)
  matrix products  128 us (18%)
  other arithmetic  71 us (10%)
  loops' own time  14.8 us (2%)
  starting transfers between devices  11.2 us (2%)
    ppermute x2, waiting for transfers between devices, with_halo(): lax.ppermute(head, axis, [((i + 1) % count, i) for i in range(count)])  198 us
    dot_general x8, matrix products, one_momentum(): jnp.einsum('teajrxz,tajwz->earxw', left_products, coupling, preferred_ele...  102 us
    gather x32, local copies, waits for them, and re-layouts  71.7 us
    gather x8, local copies, waits for them, and re-layouts, one_momentum(): picked = jnp.take(chosen, cluster_rows, axis=2)  70.4 us
    ppermute x2, waiting for transfers between devices, with_halo(): lax.ppermute(tail, axis, [(i, (i + 1) % count) for i in range(count)])  70.3 us
    select_n x16, other arithmetic, one_momentum(): chosen = jnp.take(window, mom_rows[moment_index], axis=0)  49 us
    dot_general x1, matrix products, per_device(): jnp.einsum('es,ksarxw->kearxw', spread, joined, precision=lax.Precision.H...  25.8 us
    gather x4, local copies, waits for them, and re-layouts, one_momentum(): chosen = jnp.take(window, mom_rows[moment_index], axis=0)  25.6 us
  transfers between devices with their start and end apart: 5, of which 4 were waited for; matrix products, arithmetic and copies ran while one was open for 34% of the time, Pallas kernels for 0%

commit v1 on v0

v1 whole, which is shorter than its diff:
```python
import functools

import jax
import jax.numpy as jnp
from jax import lax
from jax.experimental import pallas as pl
from jax.experimental.pallas import tpu as pltpu
from jax.sharding import PartitionSpec as P

REACH = 2
OFFMAX = 2
MESH = pl.DeviceIdType.MESH
PAIR = 2


def kernel(dims, counts, *refs):
    mom_local, energy_local, cluster_local, parts, size, branches, bonds, phonons = dims
    mom_count, en_count, atom_count = counts
    green, coupling, neighbours, shift, offset, weight, out = refs[:7]
    ext = refs[7 : 7 + energy_local]
    (
        couple, couple_t, left, terms, upper, lower, stage,
        own_sem, load_sem, send_sem, recv_sem, up_send, up_recv, out_sem,
    ) = refs[7 + energy_local :]
    pairs = branches * bonds
    mom = lax.axis_index("mom")
    en = lax.axis_index("en")
    atom = lax.axis_index("atom")
    mom_next = {"mom": lax.rem(mom + 1, mom_count)}
    mom_prev = {"mom": lax.rem(mom + mom_count - 1, mom_count)}
    atom_next = {"atom": lax.rem(atom + 1, atom_count)}
    atom_prev = {"atom": lax.rem(atom + atom_count - 1, atom_count)}
    en_next = {"en": lax.rem(en + 1, en_count)}
    en_prev = {"en": lax.rem(en + en_count - 1, en_count)}

    barrier = pltpu.get_barrier_semaphore()
    for device in (mom_next, mom_prev, atom_next, atom_prev, en_next, en_prev):
        pl.semaphore_signal(barrier, inc=1, device_id=device, device_id_type=MESH)
    pl.semaphore_wait(barrier, 6)

    def remote(e, slot, source, target, device):
        return pltpu.make_async_remote_copy(
            src_ref=source,
            dst_ref=target,
            send_sem=send_sem.at[e, slot],
            recv_sem=recv_sem.at[e, slot],
            device_id=device,
            device_id_type=MESH,
        )

    low = pl.ds(0, REACH)
    mid_k = pl.ds(REACH, mom_local)
    mid_a = pl.ds(REACH, cluster_local)
    high_k = pl.ds(REACH + mom_local, REACH)
    high_a = pl.ds(REACH + cluster_local, REACH)
    last_a = pl.ds(cluster_local, REACH)
    first_a = pl.ds(REACH, REACH)

    own = [
        pltpu.make_async_copy(green.at[:, e], ext[e].at[mid_k, mid_a], own_sem.at[e])
        for e in range(energy_local)
    ]
    mom_copies = [
        (
            remote(e, 0, green.at[pl.ds(mom_local - REACH, REACH), e], ext[e].at[low, mid_a], mom_next),
            remote(e, 1, green.at[low, e], ext[e].at[high_k, mid_a], mom_prev),
        )
        for e in range(energy_local)
    ]
    atom_copies = [
        (
            remote(e, 2, green.at[:, e, pl.ds(cluster_local - REACH, REACH)], ext[e].at[mid_k, low], atom_next),
            remote(e, 3, green.at[:, e, low], ext[e].at[mid_k, high_a], atom_prev),
        )
        for e in range(energy_local)
    ]
    corner_copies = [
        (
            remote(e, 4, ext[e].at[low, last_a], ext[e].at[low, low], atom_next),
            remote(e, 5, ext[e].at[low, first_a], ext[e].at[low, high_a], atom_prev),
            remote(e, 6, ext[e].at[high_k, last_a], ext[e].at[high_k, low], atom_next),
            remote(e, 7, ext[e].at[high_k, first_a], ext[e].at[high_k, high_a], atom_prev),
        )
        for e in range(energy_local)
    ]
    up_copies = [
        pltpu.make_async_remote_copy(
            src_ref=upper.at[i],
            dst_ref=lower.at[i],
            send_sem=up_send.at[i],
            recv_sem=up_recv.at[i],
            device_id=en_next,
            device_id_type=MESH,
        )
        for i in range(OFFMAX)
    ]
    out_copies = [None] * energy_local

    order = list(range(energy_local - OFFMAX, energy_local)) + list(range(energy_local - OFFMAX))
    for e in order:
        for copy in mom_copies[e]:
            copy.start()
        if e == order[0]:
            for copy in atom_copies[e]:
                copy.start()
    load = pltpu.make_async_copy(coupling, couple, load_sem)
    load.start()
    for e in order:
        own[e].start()
    for copy in atom_copies[order[1]]:
        copy.start()
    load.wait()

    def transpose_one(index, carry):
        a = index // pairs
        p = index % pairs
        row = pl.multiple_of(p * size, size)
        couple_t[a, pl.ds(row, size), :] = couple[p // bonds, a, p % bonds].T
        return carry

    lax.fori_loop(0, cluster_local * pairs, transpose_one, 0)

    mix = []
    for distance in range(1, OFFMAX + 1):
        total = jnp.float32(0.0)
        for w in range(phonons):
            total = total + jnp.where(offset[w] == distance, weight[w], jnp.float32(0.0))
        mix.append(total)
    keep = jnp.where(en > 0, jnp.float32(1.0), jnp.float32(0.0))
    clusters = cluster_local * atom_count
    groups = mom_local // PAIR

    def compute(e):
        def one(index, carry):
            a = index // groups
            k0 = (index % groups) * PAIR
            cluster = atom * cluster_local + a
            nears = [
                jnp.minimum(
                    lax.rem(neighbours[a * bonds + j] - cluster + REACH + clusters, clusters), 2 * REACH
                )
                + a
                for j in range(bonds)
            ]
            for p in range(pairs):
                t, j = divmod(p, bonds)
                near = nears[j]
                for step in range(PAIR):
                    block = ext[e][k0 + step + REACH - shift[t], near]
                    both = jnp.concatenate([block[0], block[1]], axis=1)
                    product = jnp.dot(
                        couple[t, a, j], both, preferred_element_type=jnp.float32
                    ).astype(jnp.bfloat16)
                    for part in range(parts):
                        left[pl.ds((step * parts + part) * size, size), pl.ds(p * size, size)] = product[
                            :, part * size : (part + 1) * size
                        ]
            result = jnp.dot(left[...], couple_t[a], preferred_element_type=jnp.float32)
            result = result.reshape(PAIR, parts, size, size)
            for step in range(PAIR):
                terms[e, k0 + step, a] = result[step]
                if e >= energy_local - OFFMAX:
                    upper[e - (energy_local - OFFMAX), k0 + step, a] = result[step].astype(jnp.bfloat16)
            return carry

        lax.fori_loop(0, cluster_local * groups, one, 0)

    started = []

    def emit(e):
        if len(started) >= 2:
            out_copies[started[-2]].wait()
        slot = len(started) % 2
        started.append(e)
        out_copies[e] = pltpu.make_async_copy(stage.at[slot], out.at[:, e], out_sem.at[e])

        def source(distance, k, a):
            if e - distance >= 0:
                return terms[e - distance, k, a] * mix[distance - 1]
            return lower[OFFMAX + e - distance, k, a].astype(jnp.float32) * (keep * mix[distance - 1])

        def one(index, carry):
            k = index // cluster_local
            a = index % cluster_local
            total = source(1, k, a)
            for distance in range(2, OFFMAX + 1):
                total = total + source(distance, k, a)
            stage[slot, k, a] = total
            return carry

        lax.fori_loop(0, mom_local * cluster_local, one, 0)
        out_copies[e].start()

    def finish(i):
        e = order[i]
        own[e].wait()
        for copy in atom_copies[e] + corner_copies[e]:
            copy.wait_recv()
        compute(e)

    done = set()

    def emit_ready(through):
        have = set(order[: through + 1])
        for e in range(OFFMAX, energy_local):
            if e not in done and all(e - d in have for d in range(1, OFFMAX + 1)):
                done.add(e)
                emit(e)

    for i, e in enumerate(order):
        for copy in mom_copies[e]:
            copy.wait_recv()
        for copy in corner_copies[e]:
            copy.start()
        if i + 2 < energy_local:
            for copy in atom_copies[order[i + 2]]:
                copy.start()
        if 2 <= i < 2 + OFFMAX:
            up_copies[i - 2].start()
        if i >= 1:
            finish(i - 1)
            emit_ready(i - 1)
    for copy in up_copies:
        copy.wait_recv()
    for e in range(OFFMAX):
        emit(e)
    finish(energy_local - 1)
    emit_ready(energy_local - 1)
    for e in started[-2:]:
        out_copies[e].wait()
    for e in range(energy_local):
        for copy in mom_copies[e] + atom_copies[e] + corner_copies[e]:
            copy.wait_send()
    for copy in up_copies:
        copy.wait_send()


def per_device(green, coupling, neighbours, shift, offset, weight):
    mom_local, energy_local, cluster_local, parts, size, _ = green.shape
    branches, _, bonds = coupling.shape[:3]
    phonons = offset.shape[0]
    pairs = branches * bonds
    counts = tuple(lax.axis_size(name) for name in ("mom", "en", "atom"))
    dims = (mom_local, energy_local, cluster_local, parts, size, branches, bonds, phonons)
    extended = (mom_local + 2 * REACH, cluster_local + 2 * REACH, parts, size, size)
    block = (mom_local, cluster_local, parts, size, size)
    smem = pl.BlockSpec(memory_space=pltpu.SMEM)
    hbm = pl.BlockSpec(memory_space=pl.ANY)
    dma = pltpu.SemaphoreType.DMA
    return pl.pallas_call(
        functools.partial(kernel, dims, counts),
        out_shape=jax.ShapeDtypeStruct(green.shape, jnp.float32),
        in_specs=[hbm, hbm, smem, smem, smem, smem],
        out_specs=hbm,
        scratch_shapes=[pltpu.VMEM(extended, jnp.bfloat16) for _ in range(energy_local)]
        + [
            pltpu.VMEM(coupling.shape, jnp.bfloat16),
            pltpu.VMEM((cluster_local, pairs * size, size), jnp.bfloat16),
            pltpu.VMEM((PAIR * parts * size, pairs * size), jnp.bfloat16),
            pltpu.VMEM((energy_local,) + block, jnp.float32),
            pltpu.VMEM((OFFMAX,) + block, jnp.bfloat16),
            pltpu.VMEM((OFFMAX,) + block, jnp.bfloat16),
            pltpu.VMEM((2,) + block, jnp.float32),
            dma((energy_local,)),
            dma,
            dma((energy_local, 8)),
            dma((energy_local, 8)),
            dma((OFFMAX,)),
            dma((OFFMAX,)),
            dma((energy_local,)),
        ],
        compiler_params=pltpu.CompilerParams(
            collective_id=0, has_side_effects=True, vmem_limit_bytes=67043328
        ),
    )(green, coupling, neighbours.reshape(-1), shift, offset, weight)


def solution(mesh):
    return jax.shard_map(
        per_device,
        mesh=mesh,
        in_specs=(
            P("mom", "en", "atom", None, None, None),
            P(None, "atom", None, None, None),
            P("atom", None),
            P(),
            P(),
            P(),
        ),
        out_specs=P("mom", "en", "atom", None, None, None),
        check_vma=False,
    )
```

time: 721 us -> 182 us (0.25)
  waiting for transfers between devices: 268 us -> 0 us
  local copies, waits for them, and re-layouts: 225 us -> 12.8 us
  Pallas kernels: 0 us -> 169 us
  matrix products: 128 us -> 0 us
  other arithmetic: 71 us -> 0 us
  loops' own time: 14.8 us -> 0 us
  starting transfers between devices: 11.2 us -> 0 us
    ppermute x5 -> x0, waiting for transfers between devices: 268 us -> none  [the longest x2 198 us: with_halo(): lax.ppermute(head, axis, [((i + 1) % count, i) for i in range(count)])]
    pallas_call x0 -> x1, Pallas kernels: none -> 169 us  [per_device(): pl.pallas_call(functools.partial(kernel, dims, counts), out_shape=jax.Sha...]
    gather x44 -> x0, local copies, waits for them, and re-layouts: 168 us -> none
    dot_general x9 -> x0, matrix products: 128 us -> none  [the longest x8 102 us: one_momentum(): jnp.einsum('teajrxz,tajwz->earxw', left_products, coupling, preferred_ele...]
    select_n x24 -> x0, other arithmetic: 49 us -> none  [the longest x16 49 us: one_momentum(): chosen = jnp.take(window, mom_rows[moment_index], axis=0)]
    dynamic_update_slice x8 -> x0, local copies, waits for them, and re-layouts: 18 us -> none  [block_terms(): return lax.map(one_momentum, jnp.arange(mom_rows.shape[0], dtype=jnp.int32))]
    another operation x6 -> x0, loops' own time: 14.8 us -> none  [the longest x2 14.7 us: block_terms(): return lax.map(one_momentum, jnp.arange(mom_rows.shape[0], dtype=jnp.int32))]
    concatenate x1 -> x0, other arithmetic: 13.8 us -> none  [with_halo(): jnp.concatenate([lax.ppermute(tail, axis, [(i, (i + 1) % count) for i in...]
  transfers between devices with their start and end apart: 5 -> 0, of which waited for: 4 -> 0; matrix products, arithmetic and copies ran while one was open for 34% -> 0% of each run, Pallas kernels for 0% -> 0%
where the time goes in v1:
time: 182 us
  Pallas kernels  169 us (93%)
  local copies, waits for them, and re-layouts  12.8 us (7%)
    pallas_call x1, Pallas kernels, per_device(): pl.pallas_call(functools.partial(kernel, dims, counts), out_shape=jax.Sha...  169 us
    unnamed x1, local copies, waits for them, and re-layouts  11.5 us

profile of v1, /device:TPU:0, one launch (start us, length us, event | category | flops | bytes accessed | tf_op | source)
XLA Modules:
  0.0 182.0 jit_solution(11629053594326370108)
XLA Ops:
  0.0 1.3 reshape.3.refs_2_
  1.3 169.1 %shard_map.64 = f32[4,6,4,2,128,128]{5,4,3,2,1,0:T(8,128)} custom-call(bf16[4,6,4,2,128,128]{5,4,3,2,1,0:T(8,128)(2,1)} %refs_0_.1, bf16[4,4,4,128,128]{4,3,2,1,0:T(8,128)(2,1)} %refs_1_.1, s32[16]{0:T(128)} %reshape.3.refs_2_, s32[4]{0:T(128)} %refs_3_.1, s32[4]{0:T(128)} %refs_4_.1, f32[4]{0:T(128)} %refs_5_.1), custom_call_target="tpu_custom_call" | custom-call | tf_op jit(solution)/shard_map/pallas_call | solution.py:250
  170.4 11.5 %copy.8 = f32[4,6,4,2,128,128]{5,4,3,2,1,0:T(8,128)} copy(f32[4,6,4,2,128,128]{5,4,3,2,1,0:T(8,128)} %shard_map.64) | data formatting | bytes 25165824

commit v2 on v1

v2 whole, which is shorter than its diff:
```python
import functools

import jax
import jax.numpy as jnp
from jax import lax
from jax.experimental import pallas as pl
from jax.experimental.pallas import tpu as pltpu
from jax.sharding import PartitionSpec as P

REACH = 2
OFFMAX = 2
MESH = pl.DeviceIdType.MESH
PAIR = 2


def kernel(dims, counts, *refs):
    mom_local, energy_local, cluster_local, parts, size, branches, bonds, phonons = dims
    mom_count, en_count, atom_count = counts
    units = energy_local * parts
    kept = parts // 2
    top = energy_local - 1
    green, coupling, neighbours, shift, offset, weight, out = refs[:7]
    ext = refs[7 : 7 + units]
    (
        couple, couple_t, left, terms, upper, lower, stage,
        own_sem, load_sem, send_sem, recv_sem, up_send, up_recv, pass_send, pass_recv, out_sem,
    ) = refs[7 + units :]
    pairs = branches * bonds
    mom = lax.axis_index("mom")
    en = lax.axis_index("en")
    atom = lax.axis_index("atom")
    mom_next = {"mom": lax.rem(mom + 1, mom_count)}
    mom_prev = {"mom": lax.rem(mom + mom_count - 1, mom_count)}
    atom_next = {"atom": lax.rem(atom + 1, atom_count)}
    atom_prev = {"atom": lax.rem(atom + atom_count - 1, atom_count)}
    en_next = {"en": lax.rem(en + 1, en_count)}
    en_prev = {"en": lax.rem(en + en_count - 1, en_count)}
    has_next = en < en_count - 1
    has_prev = en > 0

    barrier = pltpu.get_barrier_semaphore()
    for device in (mom_next, mom_prev, atom_next, atom_prev, en_next, en_prev):
        pl.semaphore_signal(barrier, inc=1, device_id=device, device_id_type=MESH)
    pl.semaphore_wait(barrier, 6)

    low = pl.ds(0, REACH)
    mid_k = pl.ds(REACH, mom_local)
    mid_a = pl.ds(REACH, cluster_local)
    high_k = pl.ds(REACH + mom_local, REACH)
    high_a = pl.ds(REACH + cluster_local, REACH)
    last_k = pl.ds(mom_local, REACH)
    last_a = pl.ds(cluster_local, REACH)
    first = pl.ds(REACH, REACH)
    tail_k = pl.ds(mom_local - REACH, REACH)
    tail_a = pl.ds(cluster_local - REACH, REACH)

    def energy_part(u):
        return divmod(u, parts)

    def guarded(u, body):
        e, part = energy_part(u)
        if e < top:
            body()
        elif part < kept:
            pl.when(has_next)(body)
        else:
            pl.when(has_prev)(body)

    def passed(u):
        e, part = energy_part(u)
        return e == top and part >= kept

    def remote(u, slot, source, target, device):
        return pltpu.make_async_remote_copy(
            src_ref=source,
            dst_ref=target,
            send_sem=send_sem.at[u, slot],
            recv_sem=recv_sem.at[u, slot],
            device_id=device,
            device_id_type=MESH,
        )

    def own_copy(u):
        e, part = energy_part(u)
        return pltpu.make_async_copy(green.at[:, e, :, part], ext[u].at[mid_k, mid_a], own_sem.at[u])

    def pass_copy(u):
        e, part = energy_part(u)
        return pltpu.make_async_remote_copy(
            src_ref=green.at[:, e, :, part],
            dst_ref=ext[u].at[mid_k, mid_a],
            send_sem=pass_send.at[part - kept],
            recv_sem=pass_recv.at[part - kept],
            device_id=en_next,
            device_id_type=MESH,
        )

    def mom_copies(u):
        e, part = energy_part(u)
        if passed(u):
            tail, head = ext[u].at[last_k, mid_a], ext[u].at[first, mid_a]
        else:
            tail, head = green.at[tail_k, e, :, part], green.at[low, e, :, part]
        return (
            remote(u, 0, tail, ext[u].at[low, mid_a], mom_next),
            remote(u, 1, head, ext[u].at[high_k, mid_a], mom_prev),
        )

    def atom_copies(u):
        e, part = energy_part(u)
        if passed(u):
            tail, head = ext[u].at[mid_k, last_a], ext[u].at[mid_k, first]
        else:
            tail, head = green.at[:, e, tail_a, part], green.at[:, e, low, part]
        return (
            remote(u, 2, tail, ext[u].at[mid_k, low], atom_next),
            remote(u, 3, head, ext[u].at[mid_k, high_a], atom_prev),
        )

    def corner_copies(u):
        return (
            remote(u, 4, ext[u].at[low, last_a], ext[u].at[low, low], atom_next),
            remote(u, 5, ext[u].at[low, first], ext[u].at[low, high_a], atom_prev),
            remote(u, 6, ext[u].at[high_k, last_a], ext[u].at[high_k, low], atom_next),
            remote(u, 7, ext[u].at[high_k, first], ext[u].at[high_k, high_a], atom_prev),
        )

    def start(copies):
        for copy in copies:
            copy.start()

    def wait_recv(copies):
        for copy in copies:
            copy.wait_recv()

    def up_copy(i):
        return pltpu.make_async_remote_copy(
            src_ref=upper.at[i],
            dst_ref=lower.at[i],
            send_sem=up_send.at[i],
            recv_sem=up_recv.at[i],
            device_id=en_next,
            device_id_type=MESH,
        )

    whole = [(top - 1) * parts + part for part in range(parts)]
    stay = [top * parts + part for part in range(kept)]
    moved = [top * parts + part for part in range(kept, parts)]
    others = list(range((top - 1) * parts))
    order = whole + stay + others[:parts] + moved + others[parts:]
    messages = whole + stay
    ahead = 4

    def start_moms(u):
        def body():
            if passed(u):
                pass_copy(u).wait_recv()
            start(mom_copies(u))

        guarded(u, body)

    for u in order[:2]:
        start_moms(u)
    for u in moved:
        pl.when(has_next)(lambda u=u: pass_copy(u).start())
    guarded(order[0], lambda: start(atom_copies(order[0])))
    for u in order[2:ahead]:
        start_moms(u)
    load = pltpu.make_async_copy(coupling, couple, load_sem)
    load.start()
    for u in order:
        if not passed(u):
            guarded(u, lambda u=u: own_copy(u).start())
    guarded(order[1], lambda: start(atom_copies(order[1])))
    load.wait()

    def transpose_one(index, carry):
        a = index // pairs
        p = index % pairs
        row = pl.multiple_of(p * size, size)
        couple_t[a, pl.ds(row, size), :] = couple[p // bonds, a, p % bonds].T
        return carry

    lax.fori_loop(0, cluster_local * pairs, transpose_one, 0)

    @pl.when(jnp.logical_not(has_prev))
    def _():
        def clear(index, carry):
            k = index // cluster_local
            a = index % cluster_local
            for i in range(len(messages)):
                lower[i, k, a] = jnp.zeros((size, size), jnp.bfloat16)
            for part in range(kept, parts):
                terms[0, part, k, a] = jnp.zeros((size, size), jnp.float32)
            return carry

        lax.fori_loop(0, mom_local * cluster_local, clear, 0)

    mix = []
    for distance in range(1, OFFMAX + 1):
        total = jnp.float32(0.0)
        for w in range(phonons):
            total = total + jnp.where(offset[w] == distance, weight[w], jnp.float32(0.0))
        mix.append(total)
    clusters = cluster_local * atom_count
    groups = mom_local // PAIR

    def compute(u):
        e, part = energy_part(u)

        def one(index, carry):
            a = index // groups
            k0 = (index % groups) * PAIR
            cluster = atom * cluster_local + a
            nears = [
                jnp.minimum(
                    lax.rem(neighbours[a * bonds + j] - cluster + REACH + clusters, clusters), 2 * REACH
                )
                + a
                for j in range(bonds)
            ]
            for p in range(pairs):
                t, j = divmod(p, bonds)
                row = k0 + REACH - shift[t]
                both = jnp.concatenate([ext[u][row + step, nears[j]] for step in range(PAIR)], axis=1)
                product = jnp.dot(
                    couple[t, a, j], both, preferred_element_type=jnp.float32
                ).astype(jnp.bfloat16)
                for step in range(PAIR):
                    left[pl.ds(step * size, size), pl.ds(p * size, size)] = product[
                        :, step * size : (step + 1) * size
                    ]
            result = jnp.dot(left[...], couple_t[a], preferred_element_type=jnp.float32)
            for step in range(PAIR):
                block = result[step * size : (step + 1) * size]
                if e < top:
                    terms[e + 1, part, k0 + step, a] = block
                elif part >= kept:
                    terms[0, part, k0 + step, a] = block
                if u in messages:
                    upper[messages.index(u), k0 + step, a] = block.astype(jnp.bfloat16)
            return carry

        lax.fori_loop(0, cluster_local * groups, one, 0)

    started = []

    def out_copy(slot, e, part):
        return pltpu.make_async_copy(stage.at[slot], out.at[:, e, :, part], out_sem.at[slot])

    def emit(e, part):
        slot = len(started) % 2
        if len(started) >= 2:
            out_copy(slot, *started[-2]).wait()
        started.append((e, part))

        def source(before, k, a):
            if before >= 0:
                return terms[before + 1, part, k, a]
            if before == -1:
                if part >= kept:
                    return terms[0, part, k, a]
                return lower[parts + part, k, a].astype(jnp.float32)
            return lower[part, k, a].astype(jnp.float32)

        def one(index, carry):
            k = index // cluster_local
            a = index % cluster_local
            total = source(e - 1, k, a) * mix[0]
            for distance in range(2, OFFMAX + 1):
                total = total + source(e - distance, k, a) * mix[distance - 1]
            stage[slot, k, a] = total
            return carry

        lax.fori_loop(0, mom_local * cluster_local, one, 0)
        out_copy(slot, e, part).start()

    def finish(i):
        u = order[i]

        def body():
            if not passed(u):
                own_copy(u).wait()
            wait_recv(atom_copies(u) + corner_copies(u))
            compute(u)

        guarded(u, body)

    done = set()

    def emit_ready(through):
        have = set(order[: through + 1])
        for e in range(OFFMAX, energy_local):
            for part in range(parts):
                if (e, part) not in done and all(
                    (e - d) * parts + part in have for d in range(1, OFFMAX + 1)
                ):
                    done.add((e, part))
                    emit(e, part)

    for i, u in enumerate(order):

        def step(u=u):
            wait_recv(mom_copies(u))
            start(corner_copies(u))

        guarded(u, step)
        if i + ahead < units:
            start_moms(order[i + ahead])
        if i + 2 < units:
            guarded(order[i + 2], lambda v=order[i + 2]: start(atom_copies(v)))
        if 2 <= i < 2 + len(messages):
            pl.when(has_next)(lambda i=i: up_copy(i - 2).start())
        if i >= 1:
            finish(i - 1)
            emit_ready(i - 1)
        if i == units - 2:

            @pl.when(has_prev)
            def _():
                for n in range(len(messages)):
                    up_copy(n).wait_recv()

            for e in range(OFFMAX):
                for part in range(parts):
                    emit(e, part)
    finish(units - 1)
    emit_ready(units - 1)
    for n in (2, 1):
        out_copy((len(started) - n) % 2, *started[-n]).wait()
    for u in order:

        def drain(u=u):
            for copy in mom_copies(u) + atom_copies(u) + corner_copies(u):
                copy.wait_send()

        guarded(u, drain)

    @pl.when(has_next)
    def _():
        for n in range(len(messages)):
            up_copy(n).wait_send()
        for u in moved:
            pass_copy(u).wait_send()


def per_device(green, coupling, neighbours, shift, offset, weight):
    mom_local, energy_local, cluster_local, parts, size, _ = green.shape
    branches, _, bonds = coupling.shape[:3]
    phonons = offset.shape[0]
    pairs = branches * bonds
    counts = tuple(lax.axis_size(name) for name in ("mom", "en", "atom"))
    dims = (mom_local, energy_local, cluster_local, parts, size, branches, bonds, phonons)
    extended = (mom_local + 2 * REACH, cluster_local + 2 * REACH, size, size)
    block = (mom_local, cluster_local, size, size)
    units = energy_local * parts
    sent = parts + parts // 2
    smem = pl.BlockSpec(memory_space=pltpu.SMEM)
    hbm = pl.BlockSpec(memory_space=pl.ANY)
    dma = pltpu.SemaphoreType.DMA
    return pl.pallas_call(
        functools.partial(kernel, dims, counts),
        out_shape=jax.ShapeDtypeStruct(green.shape, jnp.float32),
        in_specs=[hbm, hbm, smem, smem, smem, smem],
        out_specs=hbm,
        scratch_shapes=[pltpu.VMEM(extended, jnp.bfloat16) for _ in range(units)]
        + [
            pltpu.VMEM(coupling.shape, jnp.bfloat16),
            pltpu.VMEM((cluster_local, pairs * size, size), jnp.bfloat16),
            pltpu.VMEM((PAIR * size, pairs * size), jnp.bfloat16),
            pltpu.VMEM((energy_local, parts) + block, jnp.float32),
            pltpu.VMEM((sent,) + block, jnp.bfloat16),
            pltpu.VMEM((sent,) + block, jnp.bfloat16),
            pltpu.VMEM((2,) + block, jnp.float32),
            dma((units,)),
            dma,
            dma((units, 8)),
            dma((units, 8)),
            dma((sent,)),
            dma((sent,)),
            dma((parts - parts // 2,)),
            dma((parts - parts // 2,)),
            dma((2,)),
        ],
        compiler_params=pltpu.CompilerParams(
            collective_id=0, has_side_effects=True, vmem_limit_bytes=67043328
        ),
    )(green, coupling, neighbours.reshape(-1), shift, offset, weight)


def solution(mesh):
    return jax.shard_map(
        per_device,
        mesh=mesh,
        in_specs=(
            P("mom", "en", "atom", None, None, None),
            P(None, "atom", None, None, None),
            P("atom", None),
            P(),
            P(),
            P(),
        ),
        out_specs=P("mom", "en", "atom", None, None, None),
        check_vma=False,
    )
```

time: 182 us -> 159 us (0.87)
  Pallas kernels: 169 us -> 146 us
    pallas_call x1, Pallas kernels: 169 us -> 146 us  [per_device(): pl.pallas_call(functools.partial(kernel, dims, counts), out_shape=jax.Sha...]
where the time goes in v2:
time: 159 us
  Pallas kernels  146 us (92%)
  local copies, waits for them, and re-layouts  12.8 us (8%)
    pallas_call x1, Pallas kernels, per_device(): pl.pallas_call(functools.partial(kernel, dims, counts), out_shape=jax.Sha...  146 us
    unnamed x1, local copies, waits for them, and re-layouts  11.5 us

profile of v2, /device:TPU:0, one launch (start us, length us, event | category | flops | bytes accessed | tf_op | source)
XLA Modules:
  0.0 158.9 jit_solution(12129556198470440577)
XLA Ops:
  0.0 1.3 reshape.3.refs_2_
  1.3 146.1 %shard_map.64 = f32[4,6,4,2,128,128]{5,4,3,2,1,0:T(8,128)} custom-call(bf16[4,6,4,2,128,128]{5,4,3,2,1,0:T(8,128)(2,1)} %refs_0_.1, bf16[4,4,4,128,128]{4,3,2,1,0:T(8,128)(2,1)} %refs_1_.1, s32[16]{0:T(128)} %reshape.3.refs_2_, s32[4]{0:T(128)} %refs_3_.1, s32[4]{0:T(128)} %refs_4_.1, f32[4]{0:T(128)} %refs_5_.1), custom_call_target="tpu_custom_call" | custom-call | tf_op jit(solution)/shard_map/pallas_call | solution.py:361
  147.4 11.5 %copy.8 = f32[4,6,4,2,128,128]{5,4,3,2,1,0:T(8,128)} copy(f32[4,6,4,2,128,128]{5,4,3,2,1,0:T(8,128)} %shard_map.64) | data formatting | bytes 25165824
